TPU v7x, 512 devices: a whole 4x4x16 slice. The times are simulated.
512 devices in a mesh: layer: 32 (over y, x, core), latent: 16 (over z).
Axes of the slice: x: 4, y: 4, z: 16, core: 2. Of those that a mesh axis runs over, the one named last changes fastest.
Arguments:
- layer_input: bfloat16 [32, 1024, 4096], P('layer', None, 'latent'), may hold values from -6 to 6
- enc_weight: bfloat16 [32, 4096, 2048], P('layer', None, 'latent'), may hold values from -0.09375 to 0.09375
- enc_bias: float32 [32, 2048], P('layer', 'latent'), may hold values from -3 to 3
- dec_weight: bfloat16 [32, 3, 2048, 4096], P('layer', None, None, 'latent'), may hold values from -0.25 to 0.25
- block_lists: int32 [32, 16, 8], P('layer'), may hold values from 0 to 15, as said below
- block_counts: int32 [32, 16], P('layer'), may hold values from 1 to 8, as said below
Outputs:
- rebuilt: bfloat16 [32, 1024, 4096], P('layer', None, 'latent')
Inputs may be any that keep to these rules, and one draw needn't show every extreme that they name: `block_lists`: each list holds distinct block ids of one layer. `block_counts`: some entry equals 8 in every draw.
All inputs are finite; a program needn't handle non-finite values.
Results may differ from a plain program's by a relative error of at most 0.0055.
Values may be sent and summed in bfloat16 or wider, within the bound.
A program may use at most 128 MiB of HBM per device.

v0:
```python
import jax
import jax.numpy as jnp
from jax import lax
from jax.sharding import PartitionSpec as P


def passed_along(value, axis, steps):
    count = lax.axis_size(axis)
    initial, last = (max(0, -steps), min(count, count - steps))
    return lax.ppermute(value, axis, [(source, source + steps) for source in range(initial, last)])


def shards(layer_input, enc_weight, enc_bias, dec_weight, block_lists, block_counts):
    encoder = enc_weight[0]
    tokens = layer_input.shape[1]
    block_width = encoder.shape[1]
    weight_rows = encoder
    preact = jnp.dot(
        lax.all_gather(layer_input, "latent", axis=2, tiled=True)[0],
        weight_rows,
        preferred_element_type=jnp.float32,
    )
    preact = preact + enc_bias[0][None, :]
    own_block = lax.axis_index("latent")
    active_ids = block_lists[0]
    counts = block_counts[0]
    slot_ids = jnp.arange(active_ids.shape[1])
    in_count = slot_ids[None, :] < counts[:, None]
    matched = (active_ids == own_block) & in_count
    tile_hit = jnp.any(matched, axis=1).astype(jnp.float32)
    tile_count = active_ids.shape[0]
    latent_act = (
        (
            jnp.maximum(preact, 0.0).reshape(tile_count, tokens // tile_count, block_width)
            * tile_hit[:, None, None]
        )
        .reshape(tokens, block_width)
        .astype(jnp.bfloat16)
    )
    decoder = dec_weight[0]
    targets = decoder.shape[0]
    weight_rows = decoder
    partials = jnp.einsum(
        "tk,skd->std",
        lax.all_gather(latent_act, "latent", axis=1, tiled=True),
        weight_rows,
        preferred_element_type=jnp.float32,
    )
    rebuilt = partials[0]
    for offset in range(1, targets):
        arrived = passed_along(partials[offset].astype(jnp.bfloat16), "layer", offset)
        rebuilt = rebuilt + arrived.astype(jnp.float32)
    return rebuilt.astype(jnp.bfloat16)[None]


def solution(mesh):
    placed = (
        P("layer", None, "latent"),
        P("layer", None, "latent"),
        P("layer", "latent"),
        P("layer", None, None, "latent"),
        P("layer", None, None),
        P("layer", None),
    )
    return jax.shard_map(
        shards, mesh=mesh, in_specs=placed, out_specs=P("layer", None, "latent"), check_vma=False
    )
```

profile of v0, /device:TPU:9, one launch (start us, length us, event | category | flops | bytes accessed | tf_op | source)
XLA Modules:
  0.0 277.0 jit_solution(11785571274011899842)
XLA Ops:
  6.5 0.0 copy-start
  6.5 0.0 all-gather.3.cloned.1.call-start
  6.5 0.7 all-gather.3.cloned.1.call-update
  7.3 0.0 all-gather.5.cloned.1.call-start
  7.3 0.9 fusion.28
  8.2 0.1 mul.13
  8.3 0.1 mul.14
  8.3 123.7 %all-gather.3.cloned.1.call-done = bf16[1,1024,4096]{2,1,0:T(8,128)(2,1)} async-done(((bf16[1,1024,256]{2,1,0:T(8,128)(2,1)}), bf16[1,1024,4096]{2,1,0:T(8,128)(2,1)}) %all-gather.3.cloned.1.call-update) | async-done | bytes 8388624 | tf_op jit(solution)/shard_map/all_gather | solution.py:19
  132.1 6.8 %fusion.19 = bf16[1024,128]{1,0:T(8,128)(2,1)} fusion(bf16[1,1024,4096]{2,1,0:T(8,128)(2,1)} %all-gather.3.cloned.1.call-done, bf16[1,4096,128]{2,1,0:T(8,128)(2,1)} %param.7, f32[1024]{0:T(1024)S(1)} %mul.14, f32[128]{0:T(128)} %bitcast.51), kind=kOutput, calls=%fused_computation.9 | convolution fusion | flops 1074266112 | bytes 9703936 | tf_op jit(solution)/shard_map/dot_general | solution.py:18
  138.8 0.0 all-gather.5.cloned.1.call-update
  138.9 92.0 %all-gather.5.cloned.1.call-done = bf16[1024,2048]{1,0:T(8,128)(2,1)} async-done(((bf16[1024,128]{1,0:T(8,128)(2,1)}), bf16[1024,2048]{1,0:T(8,128)(2,1)}) %all-gather.5.cloned.1.call-update) | async-done | bytes 4194320 | tf_op jit(solution)/shard_map/all_gather | solution.py:45
  230.9 0.0 copy-done
  230.9 5.2 %fusion.29 = (bf16[3,1024,256]{2,1,0:T(8,128)(2,1)S(1)}, f32[3,1024,256]{2,1,0:T(8,128)S(1)}) fusion(bf16[1,3,2048,256]{3,2,1,0:T(8,128)(2,1)S(1)} %copy-done, bf16[1024,2048]{1,0:T(8,128)(2,1)} %all-gather.5.cloned.1.call-done), kind=kOutput, calls=%fused_computation.21 | convolution fusion | flops 3222011904 | bytes 12058624 | tf_op jit(solution)/shard_map/tk,skd->std/dot_general | solution.py:43
  236.1 0.1 slice_bitcast_fusion.2
  236.2 12.8 %collective-permute-start = (bf16[1024,256]{1,0:T(8,128)(2,1)S(1)}, bf16[1024,256]{1,0:T(8,128)(2,1)S(1)}, u32[]{:S(2)}, u32[]{:S(2)}) collective-permute-start(bf16[1024,256]{1,0:T(8,128)(2,1)S(1)} %get-tuple-element.5), channel_id=1, source_target_pairs={{0,16},{16,32},{32,48},{48,64},{64,80},{80,96},{96,112},{112,128},... | collective-permute-start | bytes 1572872 | tf_op jit(solution)/shard_map/ppermute | solution.py:10
  249.0 3.1 %collective-permute-start.1 = (bf16[1024,256]{1,0:T(8,128)(2,1)S(1)}, bf16[1024,256]{1,0:T(8,128)(2,1)S(1)}, u32[]{:S(2)}, u32[]{:S(2)}) collective-permute-start(bf16[1024,256]{1,0:T(8,128)(2,1)S(1)} %get-tuple-element.6), channel_id=1, source_target_pairs={{0,32},{16,48},{32,64},{48,80},{64,96},{80,112},{96,128},{112,144}... | collective-permute-start | bytes 1572872 | tf_op jit(solution)/shard_map/ppermute | solution.py:10
  252.1 6.1 %collective-permute-done = bf16[1024,256]{1,0:T(8,128)(2,1)S(1)} collective-permute-done((bf16[1024,256]{1,0:T(8,128)(2,1)S(1)}, bf16[1024,256]{1,0:T(8,128)(2,1)S(1)}, u32[]{:S(2)}, u32[]{:S(2)}) %collective-permute-start) | collective-permute-done | bytes 524320 | tf_op jit(solution)/shard_map/ppermute | solution.py:10
  258.2 11.0 %collective-permute-done.1 = bf16[1024,256]{1,0:T(8,128)(2,1)S(1)} collective-permute-done((bf16[1024,256]{1,0:T(8,128)(2,1)S(1)}, bf16[1024,256]{1,0:T(8,128)(2,1)S(1)}, u32[]{:S(2)}, u32[]{:S(2)}) %collective-permute-start.1) | collective-permute-done | bytes 524320 | tf_op jit(solution)/shard_map/ppermute | solution.py:10
  269.2 1.0 fusion.26
  (1 shorter events, 0.0 us)
Async XLA Ops:
  6.5 224.4 %copy-start = (bf16[1,3,2048,256]{3,2,1,0:T(8,128)(2,1)S(1)}, bf16[1,3,2048,256]{3,2,1,0:T(8,128)(2,1)}, u32[]{:S(2)}) copy-start(bf16[1,3,2048,256]{3,2,1,0:T(8,128)(2,1)} %param.9) | copy-start | bytes 9437188
  6.5 125.5 %all-gather.3.cloned.1.call-start = ((), (), s32[]{:S(2)}) async-start(), calls=%async_computation | async-start | bytes 8912896 | tf_op jit(solution)/shard_map/all_gather | solution.py:19
  7.3 223.7 %all-gather.5.cloned.1.call-start = ((), (), s32[]{:S(2)}) async-start(), calls=%async_computation.1 | async-start | bytes 4456448 | tf_op jit(solution)/shard_map/all_gather | solution.py:45
  236.2 22.0 %collective-permute-start = (bf16[1024,256]{1,0:T(8,128)(2,1)S(1)}, bf16[1024,256]{1,0:T(8,128)(2,1)S(1)}, u32[]{:S(2)}, u32[]{:S(2)}) collective-permute-start(bf16[1024,256]{1,0:T(8,128)(2,1)S(1)} %get-tuple-element.5), channel_id=1, source_target_pairs={{0,16},{16,32},{32,48},{48,64},{64,80},{80,96},{96,112},{112,128},... | collective-permute-start | bytes 1572872 | tf_op jit(solution)/shard_map/ppermute | solution.py:10
  249.0 20.2 %collective-permute-start.1 = (bf16[1024,256]{1,0:T(8,128)(2,1)S(1)}, bf16[1024,256]{1,0:T(8,128)(2,1)S(1)}, u32[]{:S(2)}, u32[]{:S(2)}) collective-permute-start(bf16[1024,256]{1,0:T(8,128)(2,1)S(1)} %get-tuple-element.6), channel_id=1, source_target_pairs={{0,32},{16,48},{32,64},{48,80},{64,96},{80,112},{96,128},{112,144}... | collective-permute-start | bytes 1572872 | tf_op jit(solution)/shard_map/ppermute | solution.py:10
Sparse Core Ops, SparseCore 0:
  9.3 122.6 all-gather.2
  139.0 91.8 all-gather.4
where the time goes:
time: 277 us
  waiting for transfers between devices  234 us (84%)
  starting transfers between devices  15.9 us (6%)
  between operations  13.4 us (5%)
  matrix products  12 us (4%)
    all_gather x1, waiting for transfers between devices, shards(): lax.all_gather(layer_input, 'latent', axis=2, tiled=True)[0]  124 us
    all_gather x1, waiting for transfers between devices, shards(): lax.all_gather(latent_act, 'latent', axis=1, tiled=True)  92 us
    ppermute x2, waiting for transfers between devices, passed_along(): lax.ppermute(value, axis, [(source, source + steps) for source in range(i...  17.1 us
    ppermute x2, starting transfers between devices, passed_along(): lax.ppermute(value, axis, [(source, source + steps) for source in range(i...  15.9 us
    dot_general x1, matrix products, shards(): jnp.dot(lax.all_gather(layer_input, 'latent', axis=2, tiled=True)[0], wei...  6.77 us
  transfers between devices with their start and end apart: 4, of which 4 were waited for; matrix products, arithmetic and copies ran while one was open for 0% of the time, Pallas kernels for 0%

commit v1 on v0

--- a/solution.py
+++ b/solution.py
@@ -2,6 +2,11 @@
 import jax.numpy as jnp
 from jax import lax
 from jax.sharding import PartitionSpec as P
+
+
+def exchange_gather(x, mesh_axis, dim):
+    repeated = jnp.stack([x] * lax.axis_size(mesh_axis))
+    return jnp.concatenate(lax.all_to_all(repeated, mesh_axis, 0, 0), axis=dim)
 
 
 def passed_along(value, axis, steps):
@@ -42,7 +47,7 @@
     weight_rows = decoder
     partials = jnp.einsum(
         "tk,skd->std",
-        lax.all_gather(latent_act, "latent", axis=1, tiled=True),
+        exchange_gather(latent_act, "latent", 1),
         weight_rows,
         preferred_element_type=jnp.float32,
     )

time: 277 us -> 382 us (1.38)
  the two profiles are of different devices: /device:TPU:9 before, /device:TPU:49 now
where the time goes in v1:
time: 382 us; the launch traced here: 381 us
  blocking collectives  180 us (47%)
  waiting for transfers between devices  141 us (37%)
  starting transfers between devices  20.9 us (5%)
  between operations  13.4 us (4%)
  local copies, waits for them, and re-layouts  13 us (3%)
  matrix products  11.3 us (3%)
    all_to_all x1, blocking collectives, exchange_gather(): return jnp.concatenate(lax.all_to_all(repeated, mesh_axis, 0, 0), axis=dim)  180 us
    all_gather x1, waiting for transfers between devices, shards(): lax.all_gather(layer_input, 'latent', axis=2, tiled=True)[0]  123 us
    ppermute x2, starting transfers between devices, passed_along(): lax.ppermute(value, axis, [(source, source + steps) for source in range(i...  20.9 us
    ppermute x2, waiting for transfers between devices, passed_along(): lax.ppermute(value, axis, [(source, source + steps) for source in range(i...  17.2 us
    reshape x2, local copies, waits for them, and re-layouts, exchange_gather(): return jnp.concatenate(lax.all_to_all(repeated, mesh_axis, 0, 0), axis=dim)  12 us
  transfers between devices with their start and end apart: 3, of which 3 were waited for; matrix products, arithmetic and copies ran while one was open for 0% of the time, Pallas kernels for 0%

profile of v1, /device:TPU:49, one launch (start us, length us, event | category | flops | bytes accessed | tf_op | source)
XLA Modules:
  0.0 381.4 jit_solution(8304597818880272882)
XLA Ops:
  6.5 0.0 copy-start
  6.5 0.0 all-gather.2.cloned.1.call-start
  6.5 0.7 all-gather.2.cloned.1.call-update
  7.3 0.9 fusion.25
  8.2 0.1 mul.13
  8.3 0.1 mul.14
  8.3 123.4 %all-gather.2.cloned.1.call-done = bf16[1,1024,4096]{2,1,0:T(8,128)(2,1)} async-done(((bf16[1,1024,256]{2,1,0:T(8,128)(2,1)}), bf16[1,1024,4096]{2,1,0:T(8,128)(2,1)}) %all-gather.2.cloned.1.call-update) | async-done | bytes 8388624 | tf_op jit(solution)/shard_map/all_gather | solution.py:24
  131.7 6.1 %fusion.16 = bf16[1024,128]{1,0:T(8,128)(2,1)S(1)} fusion(bf16[1,1024,4096]{2,1,0:T(8,128)(2,1)} %all-gather.2.cloned.1.call-done, bf16[1,4096,128]{2,1,0:T(8,128)(2,1)} %param.7, f32[1024]{0:T(1024)S(1)} %mul.14, f32[128]{0:T(128)} %bitcast.47), kind=kOutput, calls=%fused_computation.8 | convolution fusion | flops 1074266112 | bytes 9703936 | tf_op jit(solution)/shard_map/dot_general | solution.py:23
  137.8 0.8 stack.2
  138.6 179.6 %all_to_all.5 = bf16[16,1024,128]{2,1,0:T(8,128)(2,1)S(1)} all-to-all(bf16[16,1024,128]{2,1,0:T(8,128)(2,1)S(1)} %stack.2), channel_id=1, replica_groups=mesh['layer'=32,'latent'=16] {'latent'}, dimensions={0} | all-to-all | bytes 8388608 | tf_op jit(solution)/shard_map/all_to_all | solution.py:9
  318.2 4.6 %copy.7 = bf16[1024,16,128]{2,1,0:T(8,128)(2,1)} copy(bf16[1024,16,128]{2,0,1:T(8,128)(2,1)S(1)} %bitcast.45) | data formatting | bytes 8388608 | tf_op jit(solution)/shard_map/reshape | solution.py:9
  322.8 7.3 %reshape.21 = bf16[1024,2048,1]{1,0,2:T(8,128)(2,1)} reshape(bf16[1024,16,128]{2,1,0:T(8,128)(2,1)} %copy.7) | data formatting | bytes 8388608 | tf_op jit(solution)/shard_map/reshape | solution.py:9
  330.1 0.0 copy-done
  330.1 5.2 %fusion.26 = (bf16[3,1024,256]{2,1,0:T(8,128)(2,1)S(1)}, f32[3,1024,256]{2,1,0:T(8,128)S(1)}) fusion(bf16[1024,2048,1]{1,0,2:T(8,128)(2,1)} %reshape.21, bf16[1,3,2048,256]{3,2,1,0:T(8,128)(2,1)S(1)} %copy-done), kind=kOutput, calls=%fused_computation.20 | convolution fusion | flops 3222011904 | bytes 12058624 | tf_op jit(solution)/shard_map/tk,skd->std/dot_general | solution.py:48
  335.3 0.1 slice_bitcast_fusion.2
  335.4 17.8 %collective-permute-start = (bf16[1024,256]{1,0:T(8,128)(2,1)S(1)}, bf16[1024,256]{1,0:T(8,128)(2,1)S(1)}, u32[]{:S(2)}, u32[]{:S(2)}) collective-permute-start(bf16[1024,256]{1,0:T(8,128)(2,1)S(1)} %get-tuple-element.5), channel_id=1, source_target_pairs={{0,16},{16,32},{32,48},{48,64},{64,80},{80,96},{96,112},{112,128},... | collective-permute-start | bytes 1572872 | tf_op jit(solution)/shard_map/ppermute | solution.py:15
  353.2 3.1 collective-permute-start.1
  356.3 6.1 %collective-permute-done = bf16[1024,256]{1,0:T(8,128)(2,1)S(1)} collective-permute-done((bf16[1024,256]{1,0:T(8,128)(2,1)S(1)}, bf16[1024,256]{1,0:T(8,128)(2,1)S(1)}, u32[]{:S(2)}, u32[]{:S(2)}) %collective-permute-start) | collective-permute-done | bytes 524320 | tf_op jit(solution)/shard_map/ppermute | solution.py:15
  362.5 11.1 %collective-permute-done.1 = bf16[1024,256]{1,0:T(8,128)(2,1)S(1)} collective-permute-done((bf16[1024,256]{1,0:T(8,128)(2,1)S(1)}, bf16[1024,256]{1,0:T(8,128)(2,1)S(1)}, u32[]{:S(2)}, u32[]{:S(2)}) %collective-permute-start.1) | collective-permute-done | bytes 524320 | tf_op jit(solution)/shard_map/ppermute | solution.py:15
  373.5 1.0 fusion.23
  (1 shorter events, 0.0 us)
Async XLA Ops:
  6.5 323.6 %copy-start = (bf16[1,3,2048,256]{3,2,1,0:T(8,128)(2,1)S(1)}, bf16[1,3,2048,256]{3,2,1,0:T(8,128)(2,1)}, u32[]{:S(2)}) copy-start(bf16[1,3,2048,256]{3,2,1,0:T(8,128)(2,1)} %param.9) | copy-start | bytes 9437188
  6.5 125.2 %all-gather.2.cloned.1.call-start = ((), (), s32[]{:S(2)}) async-start(), calls=%async_computation.1 | async-start | bytes 8912896 | tf_op jit(solution)/shard_map/all_gather | solution.py:24
  335.4 27.0 %collective-permute-start = (bf16[1024,256]{1,0:T(8,128)(2,1)S(1)}, bf16[1024,256]{1,0:T(8,128)(2,1)S(1)}, u32[]{:S(2)}, u32[]{:S(2)}) collective-permute-start(bf16[1024,256]{1,0:T(8,128)(2,1)S(1)} %get-tuple-element.5), channel_id=1, source_target_pairs={{0,16},{16,32},{32,48},{48,64},{64,80},{80,96},{96,112},{112,128},... | collective-permute-start | bytes 1572872 | tf_op jit(solution)/shard_map/ppermute | solution.py:15
  353.2 20.3 %collective-permute-start.1 = (bf16[1024,256]{1,0:T(8,128)(2,1)S(1)}, bf16[1024,256]{1,0:T(8,128)(2,1)S(1)}, u32[]{:S(2)}, u32[]{:S(2)}) collective-permute-start(bf16[1024,256]{1,0:T(8,128)(2,1)S(1)} %get-tuple-element.6), channel_id=1, source_target_pairs={{0,32},{16,48},{32,64},{48,80},{64,96},{80,112},{96,128},{112,144}... | collective-permute-start | bytes 1572872 | tf_op jit(solution)/shard_map/ppermute | solution.py:15
Sparse Core Ops, SparseCore 0:
  9.3 122.3 all-gather.1
